TPU v7x, 32 devices: a whole 2x2x4 slice. The times are simulated.
32 devices in a mesh: rows: 8 (over z, y), chan: 4 (over x, core).
Axes of the slice: x: 2, y: 2, z: 4, core: 2. Of those that a mesh axis runs over, the one named last changes fastest.
Arguments:
- radiances: float32 [16, 16384], P('chan', 'rows'), may hold values from -6 to 6
- band: int32 [16384, 1], P('rows'), may hold values from 0 to 7; in each aligned block of 2048 rows (0 to 2047, 2048 to 4095, ...) at most 512 rows name the same one
- row_in_band: int32 [16384], P('rows'), may hold values from 0 to 3
- column: int32 [16384], P('rows'), may hold values from 0 to 1439
Outputs:
- cell_count: int32 [32, 1440], P('rows')
- cell_mean: float32 [16, 32, 1440], P('chan', 'rows')
- cell_var: float32 [16, 32, 1440], P('chan', 'rows')
- cell_spread: float32 [32, 1440], P('rows')
- departure: float32 [16, 16384], P('chan', 'rows')
Inputs may be any that keep to these rules, and one draw needn't show every extreme that they name: Within each aligned block of 2048 observations (one scan-time shard) no band is named by more than 512 observations, and in some blocks one band is named by exactly 512.
All inputs are finite; a program needn't handle non-finite values.
Results may differ from a plain program's by a relative error of at most 0.0003.
Values sent between devices are 32-bit elements.
A program may use at most 64 MiB of HBM per device.

v0:
```python
import math
import jax
import jax.numpy as jnp
from jax import lax
from jax.sharding import PartitionSpec as P

CHAN = 16
COLS = 1440
ROWS_DEV = 4


def slot_ranks(dest, nrows):
    obs_dev = dest.shape[0]
    width = math.gcd(obs_dev, 128)
    nblock = obs_dev // width
    owners = jnp.arange(nrows, dtype=jnp.int32)
    hot = (dest[None, :] == owners[:, None]).astype(jnp.bfloat16).reshape(nrows, nblock, width)
    upper = (
        lax.broadcasted_iota(jnp.int32, (width, width), 0)
        <= lax.broadcasted_iota(jnp.int32, (width, width), 1)
    ).astype(jnp.bfloat16)
    inner = jnp.einsum("nbk,kj->nbj", hot, upper, preferred_element_type=jnp.float32)
    hot_float = hot.astype(jnp.float32)
    totals = jnp.sum(hot_float, axis=2)
    before = jnp.cumsum(totals, axis=1) - totals
    ranks = jnp.sum(hot_float * (inner + before[:, :, None]), axis=0).reshape(obs_dev) - 1.0
    return ranks.astype(jnp.int32)


def split_pair(values):
    high = lax.optimization_barrier(values.astype(jnp.bfloat16))
    low = (values - high.astype(jnp.float32)).astype(jnp.bfloat16)
    return (high, low)


def split_three(values):
    high = lax.optimization_barrier(values.astype(jnp.bfloat16))
    rest = values - high.astype(jnp.float32)
    middle = lax.optimization_barrier(rest.astype(jnp.bfloat16))
    low = (rest - middle.astype(jnp.float32)).astype(jnp.bfloat16)
    return (high, middle, low)


def grid_lookup(table, lat_index, col_index):
    fields, nlat, ncol = table.shape
    total = lat_index.shape[0]
    width = math.gcd(total, 2048)
    flat = table.reshape(fields * nlat, ncol)
    lat_iota = jnp.arange(nlat, dtype=jnp.int32)
    col_iota = jnp.arange(ncol, dtype=jnp.int32)

    def look_turn(turn, result):
        start = turn * width
        lat_part = lax.dynamic_slice_in_dim(lat_index, start, width, 0)
        col_part = lax.dynamic_slice_in_dim(col_index, start, width, 0)
        col_hot = (col_iota[:, None] == col_part[None, :]).astype(jnp.float32)
        picked = jnp.dot(
            flat, col_hot, precision=lax.Precision.HIGHEST, preferred_element_type=jnp.float32
        ).reshape(fields, nlat, width)
        lat_hot = (lat_iota[:, None] == lat_part[None, :]).astype(jnp.float32)
        found = jnp.sum(picked * lat_hot[None], axis=1)
        return lax.dynamic_update_slice_in_dim(result, found, start, 1)

    return lax.fori_loop(0, total // width, look_turn, jnp.zeros((fields, total), jnp.float32))


def body(radiances, band, row_in_band, column):
    nrows = lax.axis_size("rows")
    chan_dev, obs_dev = radiances.shape
    cap = 2 * obs_dev // nrows
    total_slots = nrows * cap
    dest = band[:, 0]
    slot = dest * cap + slot_ranks(dest, nrows)
    rad_high, rad_middle, rad_low = split_three(radiances)
    payload = jnp.concatenate(
        [
            rad_high,
            rad_middle,
            rad_low,
            row_in_band[None, :].astype(jnp.bfloat16),
            (column // 64)[None, :].astype(jnp.bfloat16),
            (column % 64)[None, :].astype(jnp.bfloat16),
            jnp.ones((1, obs_dev), jnp.bfloat16),
        ],
        axis=0,
    )
    nload = payload.shape[0]
    span = math.gcd(total_slots, 1024)
    slot_iota = jnp.arange(span, dtype=jnp.int32)

    def pack_turn(turn, buffer):
        start = turn * span
        hot = (slot[:, None] == (start + slot_iota)[None, :]).astype(jnp.bfloat16)
        placed_part = jnp.dot(payload, hot, preferred_element_type=jnp.float32)
        return lax.dynamic_update_slice_in_dim(buffer, placed_part, start, 1)

    placed = lax.fori_loop(
        0, total_slots // span, pack_turn, jnp.zeros((nload, total_slots), jnp.float32)
    )
    sent_values = (
        placed[0:chan_dev] + placed[chan_dev : 2 * chan_dev] + placed[2 * chan_dev : 3 * chan_dev]
    )
    base = 3 * chan_dev
    sent_cell = jnp.where(
        placed[base + 3] > 0.5,
        placed[base] * COLS + placed[base + 1] * 64.0 + placed[base + 2],
        -1.0,
    )
    packed = jnp.concatenate([sent_values, sent_cell[None, :]], axis=0).reshape(
        chan_dev + 1, nrows, cap
    )
    arrived = lax.all_to_all(packed, "rows", split_axis=1, concat_axis=1, tiled=True).reshape(
        chan_dev + 1, total_slots
    )
    values = arrived[:chan_dev]
    cell = arrived[chan_dev].astype(jnp.int32)
    lat_local = jnp.where(cell >= 0, cell // COLS, -1)
    col_local = jnp.where(cell >= 0, cell % COLS, -1)
    value_high, value_low = split_pair(values)
    square_high, square_low = split_pair(values * values)
    features = jnp.concatenate(
        [jnp.ones((1, total_slots), jnp.bfloat16), value_high, value_low, square_high, square_low],
        axis=0,
    )
    nfeat = features.shape[0]
    row_hot = (lat_local[None, :] == jnp.arange(ROWS_DEV, dtype=jnp.int32)[:, None]).astype(
        jnp.bfloat16
    )
    left = (features[:, None, :] * row_hot[None, :, :]).reshape(nfeat * ROWS_DEV, total_slots)
    block = math.gcd(total_slots, 2048)
    turns = total_slots // block
    columns_all = jnp.arange(COLS, dtype=jnp.int32)

    def accumulate(turn, acc):
        start = turn * block
        part = lax.dynamic_slice_in_dim(left, start, block, 1)
        picked = lax.dynamic_slice_in_dim(col_local, start, block, 0)
        col_hot = (picked[:, None] == columns_all[None, :]).astype(jnp.bfloat16)
        return acc + jnp.dot(part, col_hot, preferred_element_type=jnp.float32)

    sums = lax.fori_loop(0, turns, accumulate, jnp.zeros((nfeat * ROWS_DEV, COLS), jnp.float32))
    sums = sums.reshape(nfeat, ROWS_DEV, COLS)
    count = sums[0]
    first = sums[1 : 1 + chan_dev] + sums[1 + chan_dev : 1 + 2 * chan_dev]
    second = sums[1 + 2 * chan_dev : 1 + 3 * chan_dev] + sums[1 + 3 * chan_dev :]
    denom = jnp.maximum(count, 1.0)[None]
    mean = first / denom
    var = jnp.maximum(second / denom - mean * mean, 0.0)
    spread = lax.psum(jnp.sum(var, axis=0), "chan")
    scale = lax.rsqrt(1.0 + spread / CHAN)
    fields = grid_lookup(jnp.concatenate([mean, scale[None]], axis=0), lat_local, col_local)
    shifted = (values - fields[:chan_dev]) * fields[chan_dev][None, :]
    returned = lax.all_to_all(
        shifted.reshape(chan_dev, nrows, cap), "rows", split_axis=1, concat_axis=1, tiled=True
    )
    returned_flat = returned.reshape(chan_dev, total_slots)

    def unplace(turn, result):
        start = turn * span
        hot = (slot[:, None] == (start + slot_iota)[None, :]).astype(jnp.float32)
        part = lax.dynamic_slice_in_dim(returned_flat, start, span, 1)
        return result + lax.dot_general(
            part,
            hot,
            (((1,), (1,)), ((), ())),
            precision=lax.Precision.HIGHEST,
            preferred_element_type=jnp.float32,
        )

    departure = lax.fori_loop(
        0, total_slots // span, unplace, jnp.zeros((chan_dev, obs_dev), jnp.float32)
    )
    return (count.astype(jnp.int32), mean, var, spread, departure)


def solution(mesh):
    in_specs = (P("chan", "rows"), P("rows", None), P("rows"), P("rows"))
    out_specs = (
        P("rows", None),
        P("chan", "rows", None),
        P("chan", "rows", None),
        P("rows", None),
        P("chan", "rows"),
    )
    return jax.shard_map(body, mesh=mesh, in_specs=in_specs, out_specs=out_specs, check_vma=False)
```

profile of v0, /device:TPU:0, one launch (start us, length us, event | category | flops | bytes accessed | tf_op | source)
XLA Modules:
  0.0 82.0 jit_solution(14672771929657307120)
XLA Ops:
  0.6 0.8 convert_element_type.110
  1.4 0.8 fusion.46
  2.2 0.8 subtract_convert_fusion.2
  2.9 0.7 fusion.50
  3.7 0.7 convert_element_type.115
  4.4 0.7 broadcast_multiply_fusion.1
  5.1 0.8 convert_reduce_fusion
  5.9 0.2 reduce_window_sum.11
  6.1 0.9 %fusion.39 = f32[16,128]{1,0:T(8,128)S(1)} fusion(f32[8,16]{1,0:T(8,128)S(1)} %sub.41, s32[16,128]{1,0:T(8,128)} %bitcast.49), kind=kOutput, calls=%fused_computation.36 | convolution fusion | flops 4323328 | bytes 16896 | tf_op jit(solution)/shard_map/nbk,kj->nbj/dot_general | solution.py:22
  7.0 0.1 concatenate.17
  7.2 5.7 %while.56 = (s32[]{:T(128)}, f32[16,4096]{1,0:T(8,128)S(1)}, s32[2048]{0:T(1024)S(1)}, bf16[16,2048]{1,0:T(8,128)(2,1)S(1)}, s32[]{:T(128)}, /*index=5*/s32[]{:T(128)}, s32[]{:T(128)}, s32[]{:T(128)}) while((s32[]{:T(128)}, f32[16,4096]{1,0:T(8,128)S(1)}, s32[2048]{0:T(1024)S(1)}, bf16[16,2048]{1,0:T(8,128)(2,1)S(1)}, s32[]{:T(128)}, ...), condition=%wide.region_4.5_spmd.clone, body=%wide.region_3.4_spmd.clone.sunk | while | flops 69207048 | bytes 147595 | solution.py:97
  7.2 1.4 %fusion.70 = f32[16,4096]{1,0:T(8,128)S(1)} fusion(f32[16,4096]{1,0:T(8,128)S(1)} %get-tuple-element.638, s32[]{:T(128)S(6)} %select_n.104, bf16[16,2048]{1,0:T(8,128)(2,1)S(1)} %get-tuple-element.648, s32[1024]{0:T(1024)S(1)} %iota_add_fusion.4, s32[2048]{0:T(1024)S(1)} %get-tuple-element.647), kind=kOutput, calls=%fused_computation.10.clone.1 | convolution fusion | flops 69206016 | bytes 143364 | tf_op jit(solution)/shard_map/while/body/eval_jaxpr/dot_general | solution.py:94
  8.6 1.4 %fusion.70 = f32[16,4096]{1,0:T(8,128)S(1)} fusion(f32[16,4096]{1,0:T(8,128)S(1)} %get-tuple-element.638, s32[]{:T(128)S(6)} %select_n.104, bf16[16,2048]{1,0:T(8,128)(2,1)S(1)} %get-tuple-element.648, s32[1024]{0:T(1024)S(1)} %iota_add_fusion.4, s32[2048]{0:T(1024)S(1)} %get-tuple-element.647), kind=kOutput, calls=%fused_computation.10.clone.1 | convolution fusion | flops 69206016 | bytes 143364 | tf_op jit(solution)/shard_map/while/body/eval_jaxpr/dot_general | solution.py:94
  10.0 1.4 %fusion.70 = f32[16,4096]{1,0:T(8,128)S(1)} fusion(f32[16,4096]{1,0:T(8,128)S(1)} %get-tuple-element.638, s32[]{:T(128)S(6)} %select_n.104, bf16[16,2048]{1,0:T(8,128)(2,1)S(1)} %get-tuple-element.648, s32[1024]{0:T(1024)S(1)} %iota_add_fusion.4, s32[2048]{0:T(1024)S(1)} %get-tuple-element.647), kind=kOutput, calls=%fused_computation.10.clone.1 | convolution fusion | flops 69206016 | bytes 143364 | tf_op jit(solution)/shard_map/while/body/eval_jaxpr/dot_general | solution.py:94
  11.4 1.4 %fusion.70 = f32[16,4096]{1,0:T(8,128)S(1)} fusion(f32[16,4096]{1,0:T(8,128)S(1)} %get-tuple-element.638, s32[]{:T(128)S(6)} %select_n.104, bf16[16,2048]{1,0:T(8,128)(2,1)S(1)} %get-tuple-element.648, s32[1024]{0:T(1024)S(1)} %iota_add_fusion.4, s32[2048]{0:T(1024)S(1)} %get-tuple-element.647), kind=kOutput, calls=%fused_computation.10.clone.1 | convolution fusion | flops 69206016 | bytes 143364 | tf_op jit(solution)/shard_map/while/body/eval_jaxpr/dot_general | solution.py:94
  12.9 0.1 compare_select_fusion
  12.9 0.7 pad_maximum_fusion
  13.6 7.3 %all-to-all-start = ((f32[5,8,512]{2,0,1:T(8,128)}), f32[5,8,512]{2,0,1:T(8,128)S(1)}, u32[]{:S(2)}, u32[]{:S(2)}) async-start(f32[5,8,512]{2,0,1:T(8,128)} %pad_maximum_fusion), calls=%async_computation | async-start | bytes 262144 | tf_op jit(solution)/shard_map/all_to_all | solution.py:112
  20.9 7.3 %all-to-all-done = f32[5,8,512]{2,0,1:T(8,128)S(1)} async-done(((f32[5,8,512]{2,0,1:T(8,128)}), f32[5,8,512]{2,0,1:T(8,128)S(1)}, u32[]{:S(2)}, u32[]{:S(2)}) %all-to-all-start) | async-done | bytes 81952 | tf_op jit(solution)/shard_map/all_to_all | solution.py:112
  28.3 0.1 compare_reduce_fusion
  28.5 0.1 broadcast_remainder_fusion
  28.7 0.5 concatenate.21
  29.2 0.3 broadcast_multiply_fusion
  29.5 0.1 mul.121
  29.6 5.4 %while.58 = (s32[]{:T(128)}, f32[68,1440]{1,0:T(8,128)S(1)}, bf16[68,4096]{1,0:T(8,128)(2,1)S(1)}, s32[4096]{0:T(1024)S(1)}, s32[]{:T(128)}, /*index=5*/s32[]{:T(128)}, s32[]{:T(128)}, s32[]{:T(128)}) while((s32[]{:T(128)}, f32[68,1440]{1,0:T(8,128)S(1)}, bf16[68,4096]{1,0:T(8,128)(2,1)S(1)}, s32[4096]{0:T(1024)S(1)}, s32[]{:T(128)}, ...), condition=%wide.region_6.7_spmd.clone, body=%wide.region_5.6_spmd.clone.sunk | while | flops 404225280 | bytes 1153685 | solution.py:141
  29.6 2.7 %fusion.75 = f32[68,1440]{1,0:T(8,128)S(1)} fusion(s32[2048]{0:T(1024)S(1)} %dynamic_slice.52, f32[68,1440]{1,0:T(8,128)S(1)} %get-tuple-element.662, bf16[68,4096]{1,0:T(8,128)(2,1)S(1)} %get-tuple-element.671, s32[]{:T(128)S(6)} %select_n.106, pred[]{:T(512)S(6)} %compare.9), kind=kOutput, calls=%fused_computation.23.clone.1 | convolution fusion | flops 404225280 | bytes 1137157 | tf_op jit(solution)/shard_map/while/body/eval_jaxpr/dot_general | solution.py:139
  32.3 2.7 %fusion.75 = f32[68,1440]{1,0:T(8,128)S(1)} fusion(s32[2048]{0:T(1024)S(1)} %dynamic_slice.52, f32[68,1440]{1,0:T(8,128)S(1)} %get-tuple-element.662, bf16[68,4096]{1,0:T(8,128)(2,1)S(1)} %get-tuple-element.671, s32[]{:T(128)S(6)} %select_n.106, pred[]{:T(512)S(6)} %compare.9), kind=kOutput, calls=%fused_computation.23.clone.1 | convolution fusion | flops 404225280 | bytes 1137157 | tf_op jit(solution)/shard_map/while/body/eval_jaxpr/dot_general | solution.py:139
  35.1 0.6 slice_maximum_fusion
  35.7 0.7 fusion.53
  36.4 0.0 copy-start
  36.5 10.3 %psum.7 = f32[4,1440]{1,0:T(4,128)S(1)} all-reduce(f32[4,1440]{1,0:T(4,128)S(1)} %get-tuple-element.508), channel_id=1, replica_groups=mesh['rows'=8,'chan'=4] {'chan'}, use_global_device_ids=true, to_apply=%region_8.9 | all-reduce | flops 5760 | bytes 46080 | tf_op jit(solution)/shard_map/psum | solution.py:149
  46.7 0.0 copy-start.1
  46.8 0.0 copy-done
  46.9 0.5 copy-done.1
  47.3 8.0 %while.57 = (s32[]{:T(128)}, f32[5,4096]{1,0:T(8,128)S(1)}, s32[4096]{0:T(1024)S(1)}, f32[20,1440]{1,0:T(8,128)S(1)}, s32[4096]{0:T(1024)S(1)}, /*index=5*/s32[]{:T(128)}, s32[]{:T(128)}, s32[]{:T(128)}, s32[]{:T(128)}) while((s32[]{:T(128)}, f32[5,4096]{1,0:T(8,128)S(1)}, s32[4096]{0:T(1024)S(1)}, f32[20,1440]{1,0:T(8,128)S(1)}, ...), condition=%wide.region_11.12_spmd.clone, body=%wide.region_9.11_spmd.clone.sunk | while | flops 710825984 | bytes 1057431 | solution.py:64
  47.3 3.7 %fusion.72 = f32[20,2048]{1,0:T(8,128)S(1)} fusion(f32[20,1440]{1,0:T(8,128)S(1)} %get-tuple-element.698, s32[2048]{0:T(1024)S(1)} %dynamic_slice.49), kind=kOutput, calls=%fused_computation.15.clone.1 | convolution fusion | flops 710737920 | bytes 287232 | tf_op jit(solution)/shard_map/while/body/eval_jaxpr/dot_general | solution.py:57
  51.1 0.1 reshape.182
  51.2 0.1 multiply_reduce_fusion.2
  51.3 3.7 %fusion.72 = f32[20,2048]{1,0:T(8,128)S(1)} fusion(f32[20,1440]{1,0:T(8,128)S(1)} %get-tuple-element.698, s32[2048]{0:T(1024)S(1)} %dynamic_slice.49), kind=kOutput, calls=%fused_computation.15.clone.1 | convolution fusion | flops 710737920 | bytes 287232 | tf_op jit(solution)/shard_map/while/body/eval_jaxpr/dot_general | solution.py:57
  55.1 0.1 reshape.182
  55.2 0.1 multiply_reduce_fusion.2
  55.3 0.6 subtract_multiply_fusion
  56.0 3.3 %all-to-all-start.1 = ((f32[4,8,512]{2,0,1:T(4,128)}), f32[4,8,512]{2,0,1:T(4,128)S(1)}, u32[]{:S(2)}, u32[]{:S(2)}) async-start(f32[4,8,512]{2,0,1:T(4,128)} %bitcast.11), calls=%async_computation.1 | async-start | bytes 131072 | tf_op jit(solution)/shard_map/all_to_all | solution.py:153
  59.4 6.8 %all-to-all-done.1 = f32[4,8,512]{2,0,1:T(4,128)S(1)} async-done(((f32[4,8,512]{2,0,1:T(4,128)}), f32[4,8,512]{2,0,1:T(4,128)S(1)}, u32[]{:S(2)}, u32[]{:S(2)}) %all-to-all-start.1) | async-done | bytes 65568 | tf_op jit(solution)/shard_map/all_to_all | solution.py:153
  66.2 15.2 %while.59 = (s32[]{:T(128)}, f32[4,2048]{1,0:T(4,128)S(1)}, f32[4,4096]{1,0:T(4,128)S(1)}, s32[2048]{0:T(1024)S(1)}, s32[]{:T(128)}, /*index=5*/s32[]{:T(128)}, s32[]{:T(128)}, s32[]{:T(128)}) while((s32[]{:T(128)}, f32[4,2048]{1,0:T(4,128)S(1)}, f32[4,4096]{1,0:T(4,128)S(1)}, s32[2048]{0:T(1024)S(1)}, s32[]{:T(128)}, ...), condition=%wide.region_13.14_spmd.clone, body=%wide.region_12.13_spmd.clone.sunk | while | flops 102777864 | bytes 98453 | solution.py:170
  66.2 3.8 %fusion.78 = f32[4,2048]{1,0:T(4,128)S(1)} fusion(s32[1024]{0:T(1024)S(1)} %iota_add_fusion.5, s32[2048]{0:T(1024)S(1)} %get-tuple-element.723, f32[4,2048]{1,0:T(4,128)S(1)} %get-tuple-element.713, f32[4,4096]{1,0:T(4,128)S(1)} %get-tuple-element.722, s32[]{:T(128)S(6)} %select_n.107, pred[]{:T(512)S(6)} %compare.10), kind=kOutput, calls=%fused_computation.30.clone.1 | convolution fusion | flops 102776832 | bytes 94213 | tf_op jit(solution)/shard_map/while/body/eval_jaxpr/dot_general | solution.py:162
  70.0 3.8 %fusion.78 = f32[4,2048]{1,0:T(4,128)S(1)} fusion(s32[1024]{0:T(1024)S(1)} %iota_add_fusion.5, s32[2048]{0:T(1024)S(1)} %get-tuple-element.723, f32[4,2048]{1,0:T(4,128)S(1)} %get-tuple-element.713, f32[4,4096]{1,0:T(4,128)S(1)} %get-tuple-element.722, s32[]{:T(128)S(6)} %select_n.107, pred[]{:T(512)S(6)} %compare.10), kind=kOutput, calls=%fused_computation.30.clone.1 | convolution fusion | flops 102776832 | bytes 94213 | tf_op jit(solution)/shard_map/while/body/eval_jaxpr/dot_general | solution.py:162
  73.8 3.8 %fusion.78 = f32[4,2048]{1,0:T(4,128)S(1)} fusion(s32[1024]{0:T(1024)S(1)} %iota_add_fusion.5, s32[2048]{0:T(1024)S(1)} %get-tuple-element.723, f32[4,2048]{1,0:T(4,128)S(1)} %get-tuple-element.713, f32[4,4096]{1,0:T(4,128)S(1)} %get-tuple-element.722, s32[]{:T(128)S(6)} %select_n.107, pred[]{:T(512)S(6)} %compare.10), kind=kOutput, calls=%fused_computation.30.clone.1 | convolution fusion | flops 102776832 | bytes 94213 | tf_op jit(solution)/shard_map/while/body/eval_jaxpr/dot_general | solution.py:162
  77.6 3.8 %fusion.78 = f32[4,2048]{1,0:T(4,128)S(1)} fusion(s32[1024]{0:T(1024)S(1)} %iota_add_fusion.5, s32[2048]{0:T(1024)S(1)} %get-tuple-element.723, f32[4,2048]{1,0:T(4,128)S(1)} %get-tuple-element.713, f32[4,4096]{1,0:T(4,128)S(1)} %get-tuple-element.722, s32[]{:T(128)S(6)} %select_n.107, pred[]{:T(512)S(6)} %compare.10), kind=kOutput, calls=%fused_computation.30.clone.1 | convolution fusion | flops 102776832 | bytes 94213 | tf_op jit(solution)/shard_map/while/body/eval_jaxpr/dot_general | solution.py:162
  81.4 0.0 copy-start.2
  81.4 0.6 copy-done.2
  (45 shorter events, 0.6 us)
Async XLA Ops:
  13.6 14.7 %all-to-all-start = ((f32[5,8,512]{2,0,1:T(8,128)}), f32[5,8,512]{2,0,1:T(8,128)S(1)}, u32[]{:S(2)}, u32[]{:S(2)}) async-start(f32[5,8,512]{2,0,1:T(8,128)} %pad_maximum_fusion), calls=%async_computation | async-start | bytes 262144 | tf_op jit(solution)/shard_map/all_to_all | solution.py:112
  36.4 10.4 %copy-start = (f32[4,4,1440]{2,1,0:T(4,128)}, f32[4,4,1440]{2,1,0:T(4,128)S(1)}, u32[]{:S(2)}) copy-start(f32[4,4,1440]{2,1,0:T(4,128)S(1)} %get-tuple-element.510) | copy-start | bytes 276484
  46.7 0.6 copy-start.1
  56.0 10.2 %all-to-all-start.1 = ((f32[4,8,512]{2,0,1:T(4,128)}), f32[4,8,512]{2,0,1:T(4,128)S(1)}, u32[]{:S(2)}, u32[]{:S(2)}) async-start(f32[4,8,512]{2,0,1:T(4,128)} %bitcast.11), calls=%async_computation.1 | async-start | bytes 131072 | tf_op jit(solution)/shard_map/all_to_all | solution.py:153
  81.4 0.6 copy-start.2
where the time goes:
time: 82.7 us; the launch traced here: 82 us
  matrix products  34.5 us (42%)
  waiting for transfers between devices  14.2 us (17%)
  starting transfers between devices  10.7 us (13%)
  blocking collectives  10.3 us (12%)
  other arithmetic  9.1 us (11%)
  local copies, waits for them, and re-layouts  2.18 us (3%)
  between operations  0.93 us (1%)
    dot_general x4, matrix products, unplace(): lax.dot_general(part, hot, (((1,), (1,)), ((), ())), precision=lax.Precis...  15.1 us
    psum x1, blocking collectives, body(): spread = lax.psum(jnp.sum(var, axis=0), 'chan')  10.3 us
    dot_general x2, matrix products, look_turn(): jnp.dot(flat, col_hot, precision=lax.Precision.HIGHEST, preferred_element...  7.49 us
    all_to_all x1, waiting for transfers between devices, body(): lax.all_to_all(packed, 'rows', split_axis=1, concat_axis=1, tiled=True)  7.34 us
    all_to_all x1, starting transfers between devices, body(): lax.all_to_all(packed, 'rows', split_axis=1, concat_axis=1, tiled=True)  7.31 us
    all_to_all x1, waiting for transfers between devices, body(): lax.all_to_all(shifted.reshape(chan_dev, nrows, cap), 'rows', split_axis=...  6.83 us
    dot_general x4, matrix products, pack_turn(): placed_part = jnp.dot(payload, hot, preferred_element_type=jnp.float32)  5.63 us
    dot_general x2, matrix products, accumulate(): return acc + jnp.dot(part, col_hot, preferred_element_type=jnp.float32)  5.3 us
  transfers between devices with their start and end apart: 2, of which 2 were waited for; matrix products, arithmetic and copies ran while one was open for 0% of the time, Pallas kernels for 0%

commit v1 on v0

--- a/solution.py
+++ b/solution.py
@@ -150,8 +150,16 @@
     scale = lax.rsqrt(1.0 + spread / CHAN)
     fields = grid_lookup(jnp.concatenate([mean, scale[None]], axis=0), lat_local, col_local)
     shifted = (values - fields[:chan_dev]) * fields[chan_dev][None, :]
-    returned = lax.all_to_all(
-        shifted.reshape(chan_dev, nrows, cap), "rows", split_axis=1, concat_axis=1, tiled=True
+    returned = jnp.concatenate(
+        lax.all_to_all(
+            jnp.stack(
+                jnp.split(shifted.reshape(chan_dev, nrows, cap), lax.axis_size("rows"), axis=1)
+            ),
+            "rows",
+            0,
+            0,
+        ),
+        axis=1,
     )
     returned_flat = returned.reshape(chan_dev, total_slots)
 

time: 82.7 us -> 86.9 us (1.051)
  local copies, waits for them, and re-layouts: 2.18 us -> 6.93 us
    unnamed x8 -> x15, local copies, waits for them, and re-layouts: 1.1 us -> 5.26 us
where the time goes in v1:
time: 86.9 us; the launch traced here: 86.2 us
  matrix products  34.5 us (40%)
  waiting for transfers between devices  14.2 us (16%)
  starting transfers between devices  10.7 us (12%)
  blocking collectives  10.3 us (12%)
  other arithmetic  8.48 us (10%)
  local copies, waits for them, and re-layouts  6.93 us (8%)
  between operations  0.94 us (1%)
    dot_general x4, matrix products, unplace(): lax.dot_general(part, hot, (((1,), (1,)), ((), ())), precision=lax.Precis...  15.1 us
    psum x1, blocking collectives, body(): spread = lax.psum(jnp.sum(var, axis=0), 'chan')  10.3 us
    dot_general x2, matrix products, look_turn(): jnp.dot(flat, col_hot, precision=lax.Precision.HIGHEST, preferred_element...  7.49 us
    all_to_all x1, waiting for transfers between devices, body(): lax.all_to_all(packed, 'rows', split_axis=1, concat_axis=1, tiled=True)  7.34 us
    all_to_all x1, starting transfers between devices, body(): lax.all_to_all(packed, 'rows', split_axis=1, concat_axis=1, tiled=True)  7.31 us
    all_to_all x1, waiting for transfers between devices, body(): lax.all_to_all(jnp.stack(jnp.split(shifted.reshape(chan_dev, nrows, cap),...  6.83 us
    dot_general x4, matrix products, pack_turn(): placed_part = jnp.dot(payload, hot, preferred_element_type=jnp.float32)  5.63 us
    dot_general x2, matrix products, accumulate(): return acc + jnp.dot(part, col_hot, preferred_element_type=jnp.float32)  5.3 us
  transfers between devices with their start and end apart: 2, of which 2 were waited for; matrix products, arithmetic and copies ran while one was open for 0% of the time, Pallas kernels for 0%

profile of v1, /device:TPU:0, one launch (start us, length us, event | category | flops | bytes accessed | tf_op | source)
XLA Modules:
  0.0 86.2 jit_solution(13406176516432719519)
XLA Ops:
  0.6 0.8 convert_element_type.110
  1.4 0.8 fusion.46
  2.2 0.8 subtract_convert_fusion.2
  2.9 0.7 fusion.50
  3.7 0.7 convert_element_type.115
  4.4 0.7 broadcast_multiply_fusion.1
  5.1 0.8 convert_reduce_fusion
  5.9 0.2 reduce_window_sum.11
  6.1 0.9 %fusion.39 = f32[16,128]{1,0:T(8,128)S(1)} fusion(f32[8,16]{1,0:T(8,128)S(1)} %sub.41, s32[16,128]{1,0:T(8,128)} %bitcast.91), kind=kOutput, calls=%fused_computation.36 | convolution fusion | flops 4323328 | bytes 16896 | tf_op jit(solution)/shard_map/nbk,kj->nbj/dot_general | solution.py:22
  7.0 0.1 concatenate.17
  7.2 5.7 %while.56 = (s32[]{:T(128)}, f32[16,4096]{1,0:T(8,128)S(1)}, s32[2048]{0:T(1024)S(1)}, bf16[16,2048]{1,0:T(8,128)(2,1)S(1)}, s32[]{:T(128)}, /*index=5*/s32[]{:T(128)}, s32[]{:T(128)}, s32[]{:T(128)}) while((s32[]{:T(128)}, f32[16,4096]{1,0:T(8,128)S(1)}, s32[2048]{0:T(1024)S(1)}, bf16[16,2048]{1,0:T(8,128)(2,1)S(1)}, s32[]{:T(128)}, ...), condition=%wide.region_4.5_spmd.clone, body=%wide.region_3.4_spmd.clone.sunk | while | flops 69207048 | bytes 147595 | solution.py:97
  7.2 1.4 %fusion.70 = f32[16,4096]{1,0:T(8,128)S(1)} fusion(f32[16,4096]{1,0:T(8,128)S(1)} %get-tuple-element.638, s32[]{:T(128)S(6)} %select_n.104, bf16[16,2048]{1,0:T(8,128)(2,1)S(1)} %get-tuple-element.648, s32[1024]{0:T(1024)S(1)} %iota_add_fusion.4, s32[2048]{0:T(1024)S(1)} %get-tuple-element.647), kind=kOutput, calls=%fused_computation.10.clone.1 | convolution fusion | flops 69206016 | bytes 143364 | tf_op jit(solution)/shard_map/while/body/eval_jaxpr/dot_general | solution.py:94
  8.6 1.4 %fusion.70 = f32[16,4096]{1,0:T(8,128)S(1)} fusion(f32[16,4096]{1,0:T(8,128)S(1)} %get-tuple-element.638, s32[]{:T(128)S(6)} %select_n.104, bf16[16,2048]{1,0:T(8,128)(2,1)S(1)} %get-tuple-element.648, s32[1024]{0:T(1024)S(1)} %iota_add_fusion.4, s32[2048]{0:T(1024)S(1)} %get-tuple-element.647), kind=kOutput, calls=%fused_computation.10.clone.1 | convolution fusion | flops 69206016 | bytes 143364 | tf_op jit(solution)/shard_map/while/body/eval_jaxpr/dot_general | solution.py:94
  10.0 1.4 %fusion.70 = f32[16,4096]{1,0:T(8,128)S(1)} fusion(f32[16,4096]{1,0:T(8,128)S(1)} %get-tuple-element.638, s32[]{:T(128)S(6)} %select_n.104, bf16[16,2048]{1,0:T(8,128)(2,1)S(1)} %get-tuple-element.648, s32[1024]{0:T(1024)S(1)} %iota_add_fusion.4, s32[2048]{0:T(1024)S(1)} %get-tuple-element.647), kind=kOutput, calls=%fused_computation.10.clone.1 | convolution fusion | flops 69206016 | bytes 143364 | tf_op jit(solution)/shard_map/while/body/eval_jaxpr/dot_general | solution.py:94
  11.4 1.4 %fusion.70 = f32[16,4096]{1,0:T(8,128)S(1)} fusion(f32[16,4096]{1,0:T(8,128)S(1)} %get-tuple-element.638, s32[]{:T(128)S(6)} %select_n.104, bf16[16,2048]{1,0:T(8,128)(2,1)S(1)} %get-tuple-element.648, s32[1024]{0:T(1024)S(1)} %iota_add_fusion.4, s32[2048]{0:T(1024)S(1)} %get-tuple-element.647), kind=kOutput, calls=%fused_computation.10.clone.1 | convolution fusion | flops 69206016 | bytes 143364 | tf_op jit(solution)/shard_map/while/body/eval_jaxpr/dot_general | solution.py:94
  12.9 0.1 compare_select_fusion
  12.9 0.7 pad_maximum_fusion
  13.6 7.3 %all-to-all-start = ((f32[5,8,512]{2,0,1:T(8,128)}), f32[5,8,512]{2,0,1:T(8,128)S(1)}, u32[]{:S(2)}, u32[]{:S(2)}) async-start(f32[5,8,512]{2,0,1:T(8,128)} %pad_maximum_fusion), calls=%async_computation | async-start | bytes 262144 | tf_op jit(solution)/shard_map/all_to_all | solution.py:112
  20.9 7.3 %all-to-all-done = f32[5,8,512]{2,0,1:T(8,128)S(1)} async-done(((f32[5,8,512]{2,0,1:T(8,128)}), f32[5,8,512]{2,0,1:T(8,128)S(1)}, u32[]{:S(2)}, u32[]{:S(2)}) %all-to-all-start) | async-done | bytes 81952 | tf_op jit(solution)/shard_map/all_to_all | solution.py:112
  28.3 0.1 compare_reduce_fusion
  28.5 0.1 broadcast_remainder_fusion
  28.7 0.5 concatenate.21
  29.2 0.3 broadcast_multiply_fusion
  29.5 0.1 mul.121
  29.6 5.4 %while.58 = (s32[]{:T(128)}, f32[68,1440]{1,0:T(8,128)S(1)}, bf16[68,4096]{1,0:T(8,128)(2,1)S(1)}, s32[4096]{0:T(1024)S(1)}, s32[]{:T(128)}, /*index=5*/s32[]{:T(128)}, s32[]{:T(128)}, s32[]{:T(128)}) while((s32[]{:T(128)}, f32[68,1440]{1,0:T(8,128)S(1)}, bf16[68,4096]{1,0:T(8,128)(2,1)S(1)}, s32[4096]{0:T(1024)S(1)}, s32[]{:T(128)}, ...), condition=%wide.region_6.7_spmd.clone, body=%wide.region_5.6_spmd.clone.sunk | while | flops 404225280 | bytes 1153685 | solution.py:141
  29.6 2.7 %fusion.75 = f32[68,1440]{1,0:T(8,128)S(1)} fusion(s32[2048]{0:T(1024)S(1)} %dynamic_slice.52, f32[68,1440]{1,0:T(8,128)S(1)} %get-tuple-element.662, bf16[68,4096]{1,0:T(8,128)(2,1)S(1)} %get-tuple-element.671, s32[]{:T(128)S(6)} %select_n.106, pred[]{:T(512)S(6)} %compare.9), kind=kOutput, calls=%fused_computation.23.clone.1 | convolution fusion | flops 404225280 | bytes 1137157 | tf_op jit(solution)/shard_map/while/body/eval_jaxpr/dot_general | solution.py:139
  32.3 2.7 %fusion.75 = f32[68,1440]{1,0:T(8,128)S(1)} fusion(s32[2048]{0:T(1024)S(1)} %dynamic_slice.52, f32[68,1440]{1,0:T(8,128)S(1)} %get-tuple-element.662, bf16[68,4096]{1,0:T(8,128)(2,1)S(1)} %get-tuple-element.671, s32[]{:T(128)S(6)} %select_n.106, pred[]{:T(512)S(6)} %compare.9), kind=kOutput, calls=%fused_computation.23.clone.1 | convolution fusion | flops 404225280 | bytes 1137157 | tf_op jit(solution)/shard_map/while/body/eval_jaxpr/dot_general | solution.py:139
  35.1 0.6 slice_maximum_fusion
  35.7 0.7 fusion.53
  36.4 0.0 copy-start
  36.5 10.3 %psum.7 = f32[4,1440]{1,0:T(4,128)S(1)} all-reduce(f32[4,1440]{1,0:T(4,128)S(1)} %get-tuple-element.508), channel_id=1, replica_groups=mesh['rows'=8,'chan'=4] {'chan'}, use_global_device_ids=true, to_apply=%region_8.9 | all-reduce | flops 5760 | bytes 46080 | tf_op jit(solution)/shard_map/psum | solution.py:149
  46.7 0.0 copy-start.1
  46.8 0.0 copy-done
  46.9 0.5 copy-done.1
  47.3 8.0 %while.57 = (s32[]{:T(128)}, f32[5,4096]{1,0:T(8,128)S(1)}, s32[4096]{0:T(1024)S(1)}, f32[20,1440]{1,0:T(8,128)S(1)}, s32[4096]{0:T(1024)S(1)}, /*index=5*/s32[]{:T(128)}, s32[]{:T(128)}, s32[]{:T(128)}, s32[]{:T(128)}) while((s32[]{:T(128)}, f32[5,4096]{1,0:T(8,128)S(1)}, s32[4096]{0:T(1024)S(1)}, f32[20,1440]{1,0:T(8,128)S(1)}, ...), condition=%wide.region_11.12_spmd.clone, body=%wide.region_9.11_spmd.clone.sunk | while | flops 710825984 | bytes 1057431 | solution.py:64
  47.3 3.7 %fusion.72 = f32[20,2048]{1,0:T(8,128)S(1)} fusion(f32[20,1440]{1,0:T(8,128)S(1)} %get-tuple-element.698, s32[2048]{0:T(1024)S(1)} %dynamic_slice.49), kind=kOutput, calls=%fused_computation.15.clone.1 | convolution fusion | flops 710737920 | bytes 287232 | tf_op jit(solution)/shard_map/while/body/eval_jaxpr/dot_general | solution.py:57
  51.1 0.1 reshape.182
  51.2 0.1 multiply_reduce_fusion.2
  51.3 3.7 %fusion.72 = f32[20,2048]{1,0:T(8,128)S(1)} fusion(f32[20,1440]{1,0:T(8,128)S(1)} %get-tuple-element.698, s32[2048]{0:T(1024)S(1)} %dynamic_slice.49), kind=kOutput, calls=%fused_computation.15.clone.1 | convolution fusion | flops 710737920 | bytes 287232 | tf_op jit(solution)/shard_map/while/body/eval_jaxpr/dot_general | solution.py:57
  55.1 0.1 reshape.182
  55.2 0.1 multiply_reduce_fusion.2
  55.4 0.6 constant_dynamic-update-slice_fusion.8
  56.0 0.6 constant_dynamic-update-slice_fusion.7
  56.6 0.6 constant_dynamic-update-slice_fusion.6
  57.2 0.6 constant_dynamic-update-slice_fusion.5
  57.7 0.6 constant_dynamic-update-slice_fusion.4
  58.3 0.6 constant_dynamic-update-slice_fusion.3
  58.9 0.6 constant_dynamic-update-slice_fusion.2
  59.5 0.6 constant_dynamic-update-slice_fusion.1
  60.1 3.3 %all-to-all-start.1 = ((f32[8,4,1,512]{3,1,2,0:T(4,128)}), f32[8,4,1,512]{3,1,2,0:T(4,128)S(1)}, u32[]{:S(2)}, u32[]{:S(2)}) async-start(f32[8,4,1,512]{3,1,2,0:T(4,128)} %constant_dynamic-update-slice_fusion.1), calls=%async_computation.1 | async-start | bytes 131072 | tf_op jit(solution)/shard_map/all_to_all | solution.py:154
  63.5 6.8 %all-to-all-done.1 = f32[8,4,1,512]{3,1,2,0:T(4,128)S(1)} async-done(((f32[8,4,1,512]{3,1,2,0:T(4,128)}), f32[8,4,1,512]{3,1,2,0:T(4,128)S(1)}, u32[]{:S(2)}, u32[]{:S(2)}) %all-to-all-start.1) | async-done | bytes 65568 | tf_op jit(solution)/shard_map/all_to_all | solution.py:154
  70.3 15.2 %while.59 = (s32[]{:T(128)}, f32[4,2048]{1,0:T(4,128)S(1)}, f32[4,4096]{1,0:T(4,128)S(1)}, s32[2048]{0:T(1024)S(1)}, s32[]{:T(128)}, /*index=5*/s32[]{:T(128)}, s32[]{:T(128)}, s32[]{:T(128)}) while((s32[]{:T(128)}, f32[4,2048]{1,0:T(4,128)S(1)}, f32[4,4096]{1,0:T(4,128)S(1)}, s32[2048]{0:T(1024)S(1)}, s32[]{:T(128)}, ...), condition=%wide.region_13.14_spmd.clone, body=%wide.region_12.13_spmd.clone.sunk | while | flops 102777864 | bytes 98453 | solution.py:178
  70.3 3.8 %fusion.78 = f32[4,2048]{1,0:T(4,128)S(1)} fusion(s32[1024]{0:T(1024)S(1)} %iota_add_fusion.5, s32[2048]{0:T(1024)S(1)} %get-tuple-element.723, f32[4,2048]{1,0:T(4,128)S(1)} %get-tuple-element.713, f32[4,4096]{1,0:T(4,128)S(1)} %get-tuple-element.722, s32[]{:T(128)S(6)} %select_n.107, pred[]{:T(512)S(6)} %compare.10), kind=kOutput, calls=%fused_computation.30.clone.1 | convolution fusion | flops 102776832 | bytes 94213 | tf_op jit(solution)/shard_map/while/body/eval_jaxpr/dot_general | solution.py:170
  74.1 3.8 %fusion.78 = f32[4,2048]{1,0:T(4,128)S(1)} fusion(s32[1024]{0:T(1024)S(1)} %iota_add_fusion.5, s32[2048]{0:T(1024)S(1)} %get-tuple-element.723, f32[4,2048]{1,0:T(4,128)S(1)} %get-tuple-element.713, f32[4,4096]{1,0:T(4,128)S(1)} %get-tuple-element.722, s32[]{:T(128)S(6)} %select_n.107, pred[]{:T(512)S(6)} %compare.10), kind=kOutput, calls=%fused_computation.30.clone.1 | convolution fusion | flops 102776832 | bytes 94213 | tf_op jit(solution)/shard_map/while/body/eval_jaxpr/dot_general | solution.py:170
  77.9 3.8 %fusion.78 = f32[4,2048]{1,0:T(4,128)S(1)} fusion(s32[1024]{0:T(1024)S(1)} %iota_add_fusion.5, s32[2048]{0:T(1024)S(1)} %get-tuple-element.723, f32[4,2048]{1,0:T(4,128)S(1)} %get-tuple-element.713, f32[4,4096]{1,0:T(4,128)S(1)} %get-tuple-element.722, s32[]{:T(128)S(6)} %select_n.107, pred[]{:T(512)S(6)} %compare.10), kind=kOutput, calls=%fused_computation.30.clone.1 | convolution fusion | flops 102776832 | bytes 94213 | tf_op jit(solution)/shard_map/while/body/eval_jaxpr/dot_general | solution.py:170
  81.7 3.8 %fusion.78 = f32[4,2048]{1,0:T(4,128)S(1)} fusion(s32[1024]{0:T(1024)S(1)} %iota_add_fusion.5, s32[2048]{0:T(1024)S(1)} %get-tuple-element.723, f32[4,2048]{1,0:T(4,128)S(1)} %get-tuple-element.713, f32[4,4096]{1,0:T(4,128)S(1)} %get-tuple-element.722, s32[]{:T(128)S(6)} %select_n.107, pred[]{:T(512)S(6)} %compare.10), kind=kOutput, calls=%fused_computation.30.clone.1 | convolution fusion | flops 102776832 | bytes 94213 | tf_op jit(solution)/shard_map/while/body/eval_jaxpr/dot_general | solution.py:170
  85.5 0.0 copy-start.2
  85.6 0.6 copy-done.2
  (46 shorter events, 0.6 us)
Async XLA Ops:
  13.6 14.7 %all-to-all-start = ((f32[5,8,512]{2,0,1:T(8,128)}), f32[5,8,512]{2,0,1:T(8,128)S(1)}, u32[]{:S(2)}, u32[]{:S(2)}) async-start(f32[5,8,512]{2,0,1:T(8,128)} %pad_maximum_fusion), calls=%async_computation | async-start | bytes 262144 | tf_op jit(solution)/shard_map/all_to_all | solution.py:112
  36.4 10.4 %copy-start = (f32[4,4,1440]{2,1,0:T(4,128)}, f32[4,4,1440]{2,1,0:T(4,128)S(1)}, u32[]{:S(2)}) copy-start(f32[4,4,1440]{2,1,0:T(4,128)S(1)} %get-tuple-element.510) | copy-start | bytes 276484
  46.7 0.6 copy-start.1
  60.1 10.2 %all-to-all-start.1 = ((f32[8,4,1,512]{3,1,2,0:T(4,128)}), f32[8,4,1,512]{3,1,2,0:T(4,128)S(1)}, u32[]{:S(2)}, u32[]{:S(2)}) async-start(f32[8,4,1,512]{3,1,2,0:T(4,128)} %constant_dynamic-update-slice_fusion.1), calls=%async_computation.1 | async-start | bytes 131072 | tf_op jit(solution)/shard_map/all_to_all | solution.py:154
  85.5 0.6 copy-start.2
